TPU v7x, 32 devices: a whole 2x2x4 slice. The times are simulated.
32 devices in a mesh: domain: 2 (over x), fsdp: 16 (over z, y, core).
Axes of the slice: x: 2, y: 2, z: 4, core: 2. Of those that a mesh axis runs over, the one named last changes fastest.
Arguments:
- gradients: bfloat16 [2, 4, 4096, 512], P('domain', None, 'fsdp')
- row_counts: int32 [4], replicated, may hold values from 2048 to 4096, as said below
- domain_ids: int32 [2], replicated, may hold values from 0 to 7
- domain_weights: float32 [8], replicated, may hold values from 0.2 to 2
Outputs:
- updates: float32 [4, 4096, 512], P('domain', 'fsdp')
- new_weights: float32 [8], replicated
Inputs may be any that keep to these rules, and one draw needn't show every extreme that they name: `row_counts`: each matrix has 4096 or 2048 rows, and both counts occur.
All inputs are finite; a program needn't handle non-finite values.
Results may differ from a plain program's by a relative error of at most 0.0071.
Values may be sent and summed in bfloat16 or wider, within the bound.
No kernel may reach another device: no remote copies, remote signals or barrier semaphores. Data moves between devices by JAX's collectives and lax.ppermute only.
A program may use at most 64 MiB of HBM per device.

v0:
```python
import math
import jax
import jax.numpy as jnp
from jax import lax
from jax.sharding import PartitionSpec as P

NS_ITERS = 3
OWNERS = 8
COEF_A = 3.4445
COEF_B = -4.775
COEF_C = 2.0315
MUON_SCALE = 0.2
ETA = 4.0


def partner(shard, axis, stride):
    return lax.ppermute(shard, axis, [(i, i ^ 1 << stride) for i in range(lax.axis_size(axis))])


def group_mixing(domain_ids, domain_weights, kind_count):
    weight_share = domain_weights / jnp.sum(domain_weights)
    onehot = (domain_ids[:, None] == jnp.arange(kind_count, dtype=jnp.int32)[None, :]).astype(
        jnp.float32
    )
    counts = jnp.sum(onehot, axis=0)
    per_member = weight_share / jnp.maximum(counts, 1.0)
    group_mix = jnp.sum(onehot * per_member[None, :], axis=1)
    return (weight_share, onehot, counts, group_mix)


def summed_gram(iterate):
    gram_total = lax.dot_general(
        iterate, iterate, (((0,), (0,)), ((), ())), preferred_element_type=jnp.float32
    )
    for bit_pos in range(OWNERS.bit_length() - 1):
        gram_total = gram_total + partner(gram_total, "fsdp", bit_pos)
    return gram_total


def newton_steps(iterate):
    for repeat in range(NS_ITERS):
        gram_full = lax.optimization_barrier(summed_gram(iterate).astype(jnp.bfloat16))
        square = jnp.dot(gram_full, gram_full, preferred_element_type=jnp.float32)
        poly_term = (COEF_B * gram_full.astype(jnp.float32) + COEF_C * square).astype(jnp.bfloat16)
        iterate = lax.optimization_barrier(
            (
                COEF_A * iterate.astype(jnp.float32)
                + jnp.dot(iterate, poly_term, preferred_element_type=jnp.float32)
            ).astype(jnp.bfloat16)
        )
    return iterate


def share_scores(aligned, squares, norm_slots):
    return lax.psum((aligned, squares, norm_slots), ("domain", "fsdp"))


def body(gradients, row_counts, domain_ids, domain_weights):
    groups = lax.axis_size("domain")
    shards = lax.axis_size("fsdp")
    matrices = row_counts.shape[0]
    rows_src = gradients.shape[2]
    columns = gradients.shape[3]
    per_domain = matrices // groups
    sub_rows = rows_src // OWNERS
    own_rows = shards * sub_rows
    full_rows = rows_src * shards
    domain_pos = lax.axis_index("domain")
    shard_pos = lax.axis_index("fsdp")
    weight_share, onehot, counts, group_mix = group_mixing(
        domain_ids, domain_weights, domain_weights.shape[0]
    )
    blocks = lax.all_to_all(
        gradients.reshape(1, groups, per_domain, rows_src, columns),
        "domain",
        split_axis=1,
        concat_axis=0,
        tiled=True,
    )
    blocks = blocks.reshape(groups, per_domain, rows_src, columns)
    global_rows = shard_pos * rows_src + jnp.arange(rows_src, dtype=jnp.int32)
    limits = lax.dynamic_slice_in_dim(row_counts, domain_pos * per_domain, per_domain, 0)
    row_mask = (global_rows[None, :] < limits[:, None])[None, :, :, None]
    masked = jnp.where(row_mask, blocks.astype(jnp.float32), jnp.zeros((), jnp.float32))
    combined = jnp.sum(group_mix[:, None, None, None] * masked, axis=0)
    aligned = jnp.sum(masked * combined[None], axis=(1, 2, 3))
    squares = jnp.sum(masked * masked, axis=(1, 2, 3))
    block_squares = jnp.sum(combined * combined, axis=(1, 2))
    norm_slots = lax.dynamic_update_slice_in_dim(
        jnp.zeros((matrices,), jnp.float32), block_squares, domain_pos * per_domain, 0
    )
    aligned, squares, norm_slots = share_scores(aligned, squares, norm_slots)
    frob_norm = (
        jnp.sqrt(lax.dynamic_slice_in_dim(norm_slots, domain_pos * per_domain, per_domain, 0))
        + 1e-07
    )
    scaled = (combined / frob_norm[:, None, None]).astype(jnp.bfloat16)
    scaled = scaled.reshape(shards, 1, sub_rows, columns)
    start_rows = lax.all_to_all(scaled, "fsdp", split_axis=0, concat_axis=1, tiled=True)
    start_rows = lax.optimization_barrier(start_rows.reshape(own_rows, columns))
    finished = newton_steps(start_rows)
    returned = lax.all_to_all(
        finished.reshape(1, shards, sub_rows, columns),
        "fsdp",
        split_axis=1,
        concat_axis=0,
        tiled=True,
    )
    returned = returned.reshape(per_domain, rows_src, columns)
    updates = returned.astype(jnp.float32) * (MUON_SCALE * math.sqrt(full_rows))
    total_sq = jnp.sum(norm_slots)
    cosine = aligned / (jnp.sqrt(squares) * jnp.sqrt(total_sq) + 1e-06)
    score = jnp.sum(onehot * cosine[:, None], axis=0) / jnp.maximum(counts, 1.0)
    raised = weight_share * jnp.exp(ETA * score)
    return (updates, raised / jnp.sum(raised))


def solution(mesh):
    placed = (P("domain", None, "fsdp", None), P(), P(), P())
    return jax.shard_map(
        body,
        mesh=mesh,
        in_specs=placed,
        out_specs=(P("domain", "fsdp", None), P()),
        check_vma=False,
    )
```

profile of v0, /device:TPU:0, one launch (start us, length us, event | category | flops | bytes accessed | tf_op | source)
XLA Modules:
  0.0 265.7 jit_solution(6877497156156330844)
XLA Ops:
  0.6 0.0 copy-start.2
  0.6 0.0 copy-start
  0.7 0.0 copy-start.1
  0.7 4.4 %all-to-all-start = ((bf16[1,2,2,256,512]{4,3,2,0,1:T(8,128)(2,1)}), bf16[1,2,2,256,512]{4,3,2,0,1:T(8,128)(2,1)S(1)}, u32[]{:S(2)}, u32[]{:S(2)}) async-start(bf16[1,2,2,256,512]{4,3,2,0,1:T(8,128)(2,1)} %bitcast.31), calls=%async_computation | async-start | bytes 2097152 | tf_op jit(solution)/shard_map/all_to_all | solution.py:73
  5.0 0.0 copy-done.2
  5.0 0.1 convert_reduce_fusion
  5.1 0.0 copy-done
  5.1 0.6 reduce_sum.92
  5.7 0.0 copy-done.1
  5.7 0.1 dynamic_slice.6
  5.8 0.7 multiply_divide_fusion
  6.5 0.2 select_reduce_fusion.1
  6.7 0.1 broadcast_compare_fusion
  6.7 12.7 %all-to-all-done = bf16[1,2,2,256,512]{4,3,2,0,1:T(8,128)(2,1)S(1)} async-done(((bf16[1,2,2,256,512]{4,3,2,0,1:T(8,128)(2,1)}), bf16[1,2,2,256,512]{4,3,2,0,1:T(8,128)(2,1)S(1)}, u32[]{:S(2)}, u32[]{:S(2)}) %all-to-all-start) | async-done | bytes 1048608 | tf_op jit(solution)/shard_map/all_to_all | solution.py:73
  19.5 0.3 fusion.3
  19.8 0.2 multiply_reduce_fusion
  20.0 0.2 dynamic_update_slice.3
  20.2 0.7 fusion.5
  20.9 39.8 %all-reduce = (f32[4]{0:T(128)S(1)}, f32[2]{0:T(128)S(1)}, f32[2]{0:T(128)S(1)}) all-reduce(f32[4]{0:T(128)S(1)} %dynamic_update_slice.3, f32[2]{0:T(128)S(1)} %get-tuple-element.3, f32[2]{0:T(128)S(1)} %get-tuple-element.2), channel_id=1, replica_groups=mesh['domain'=2,'fsdp'=16] {'domain','fsdp'}, use_global_device_ids=true, to_apply=%region_5.6 | all-reduce | flops 8 | bytes 64 | tf_op jit(solution)/shard_map/psum | solution.py:55
  60.7 0.6 reduce_sum.100
  62.0 0.1 add_divide_fusion
  62.0 0.1 div.42
  62.1 0.1 div.43
  62.2 0.2 divide_convert_fusion
  62.4 19.5 %all_to_all.12 = bf16[16,1,32,512]{3,2,1,0:T(8,128)(2,1)S(1)} all-to-all(bf16[16,1,32,512]{3,2,1,0:T(8,128)(2,1)S(1)} %divide_convert_fusion), channel_id=1, replica_groups=mesh['domain'=2,'fsdp'=16] {'fsdp'}, dimensions={0} | all-to-all | bytes 1048576 | tf_op jit(solution)/shard_map/all_to_all | solution.py:99
  81.9 0.5 fusion.22
  82.4 0.2 collective-permute-start
  82.6 2.5 collective-permute-done
  85.1 0.2 add.76
  85.3 1.1 collective-permute-start.1
  86.4 24.2 %collective-permute-done.1 = f32[512,512]{1,0:T(8,128)S(1)} collective-permute-done((f32[512,512]{1,0:T(8,128)S(1)}, f32[512,512]{1,0:T(8,128)S(1)}, u32[]{:S(2)}, u32[]{:S(2)}) %collective-permute-start.1) | collective-permute-done | bytes 1048608 | tf_op jit(solution)/shard_map/ppermute | solution.py:17
  110.6 0.2 add.77
  110.8 1.8 collective-permute-start.2
  112.6 22.8 %collective-permute-done.2 = f32[512,512]{1,0:T(8,128)S(1)} collective-permute-done((f32[512,512]{1,0:T(8,128)S(1)}, f32[512,512]{1,0:T(8,128)S(1)}, u32[]{:S(2)}, u32[]{:S(2)}) %collective-permute-start.2) | collective-permute-done | bytes 1048608 | tf_op jit(solution)/shard_map/ppermute | solution.py:17
  135.4 0.3 add_convert_fusion.5
  135.7 0.8 fusion.6
  136.5 0.5 fusion.23
  137.0 0.1 collective-permute-start.3
  137.0 2.6 collective-permute-done.3
  139.7 0.2 add.81
  139.9 1.3 collective-permute-start.4
  141.2 23.9 %collective-permute-done.4 = f32[512,512]{1,0:T(8,128)S(1)} collective-permute-done((f32[512,512]{1,0:T(8,128)S(1)}, f32[512,512]{1,0:T(8,128)S(1)}, u32[]{:S(2)}, u32[]{:S(2)}) %collective-permute-start.4) | collective-permute-done | bytes 1048608 | tf_op jit(solution)/shard_map/ppermute | solution.py:17
  165.2 0.2 add.82
  165.4 1.8 collective-permute-start.5
  167.2 22.6 %collective-permute-done.5 = f32[512,512]{1,0:T(8,128)S(1)} collective-permute-done((f32[512,512]{1,0:T(8,128)S(1)}, f32[512,512]{1,0:T(8,128)S(1)}, u32[]{:S(2)}, u32[]{:S(2)}) %collective-permute-start.5) | collective-permute-done | bytes 1048608 | tf_op jit(solution)/shard_map/ppermute | solution.py:17
  189.8 0.3 add_convert_fusion.3
  190.0 0.8 fusion.7
  190.8 0.5 fusion.24
  191.3 0.1 collective-permute-start.6
  191.4 2.6 collective-permute-done.6
  194.0 0.2 add.86
  194.2 1.3 collective-permute-start.7
  195.6 23.9 %collective-permute-done.7 = f32[512,512]{1,0:T(8,128)S(1)} collective-permute-done((f32[512,512]{1,0:T(8,128)S(1)}, f32[512,512]{1,0:T(8,128)S(1)}, u32[]{:S(2)}, u32[]{:S(2)}) %collective-permute-start.7) | collective-permute-done | bytes 1048608 | tf_op jit(solution)/shard_map/ppermute | solution.py:17
  219.5 0.2 add.87
  219.7 1.8 collective-permute-start.8
  221.5 22.6 %collective-permute-done.8 = f32[512,512]{1,0:T(8,128)S(1)} collective-permute-done((f32[512,512]{1,0:T(8,128)S(1)}, f32[512,512]{1,0:T(8,128)S(1)}, u32[]{:S(2)}, u32[]{:S(2)}) %collective-permute-start.8) | collective-permute-done | bytes 1048608 | tf_op jit(solution)/shard_map/ppermute | solution.py:17
  244.1 0.3 add_convert_fusion.1
  244.4 1.6 fusion.8
  245.9 4.4 %all-to-all-start.2 = ((bf16[1,16,32,512]{3,2,0,1:T(8,128)(2,1)}), bf16[1,16,32,512]{3,2,0,1:T(8,128)(2,1)S(1)}, u32[]{:S(2)}, u32[]{:S(2)}) async-start(bf16[1,16,32,512]{3,2,0,1:T(8,128)(2,1)} %bitcast.5), calls=%async_computation.2 | async-start | bytes 1048576 | tf_op jit(solution)/shard_map/all_to_all | solution.py:102
  250.4 0.1 select_reduce_fusion
  250.4 1.3 fusion.21
  251.8 1.2 broadcast_divide_fusion
  253.0 11.6 %all-to-all-done.2 = bf16[1,16,32,512]{3,2,0,1:T(8,128)(2,1)S(1)} async-done(((bf16[1,16,32,512]{3,2,0,1:T(8,128)(2,1)}), bf16[1,16,32,512]{3,2,0,1:T(8,128)(2,1)S(1)}, u32[]{:S(2)}, u32[]{:S(2)}) %all-to-all-start.2) | async-done | bytes 524320 | tf_op jit(solution)/shard_map/all_to_all | solution.py:102
  264.6 1.1 convert_multiply_fusion
  (2 shorter events, 0.0 us)
Async XLA Ops:
  0.6 4.4 %copy-start.2 = (s32[2]{0:T(128)S(1)}, s32[2]{0:T(128)}, u32[]{:S(2)}) copy-start(s32[2]{0:T(128)} %param.6) | copy-start | bytes 28
  0.6 4.5 %copy-start = (f32[8]{0:T(128)S(1)}, f32[8]{0:T(128)}, u32[]{:S(2)}) copy-start(f32[8]{0:T(128)} %param.7) | copy-start | bytes 100
  0.7 5.1 %copy-start.1 = (s32[4]{0:T(128)S(1)}, s32[4]{0:T(128)}, u32[]{:S(2)}) copy-start(s32[4]{0:T(128)} %param.5) | copy-start | bytes 52
  0.7 18.8 %all-to-all-start = ((bf16[1,2,2,256,512]{4,3,2,0,1:T(8,128)(2,1)}), bf16[1,2,2,256,512]{4,3,2,0,1:T(8,128)(2,1)S(1)}, u32[]{:S(2)}, u32[]{:S(2)}) async-start(bf16[1,2,2,256,512]{4,3,2,0,1:T(8,128)(2,1)} %bitcast.31), calls=%async_computation | async-start | bytes 2097152 | tf_op jit(solution)/shard_map/all_to_all | solution.py:73
  82.4 2.7 %collective-permute-start = (f32[512,512]{1,0:T(8,128)S(1)}, f32[512,512]{1,0:T(8,128)S(1)}, u32[]{:S(2)}, u32[]{:S(2)}) collective-permute-start(f32[512,512]{1,0:T(8,128)S(1)} %fusion.22), channel_id=1, source_target_pairs={{0,1},{1,0},{2,3},{3,2},{4,5},{5,4},{6,7},{7,6},{8,9},{9,8},{10,11... | collective-permute-start | bytes 3145736 | tf_op jit(solution)/shard_map/ppermute | solution.py:17
  85.3 25.3 %collective-permute-start.1 = (f32[512,512]{1,0:T(8,128)S(1)}, f32[512,512]{1,0:T(8,128)S(1)}, u32[]{:S(2)}, u32[]{:S(2)}) collective-permute-start(f32[512,512]{1,0:T(8,128)S(1)} %add.76), channel_id=1, source_target_pairs={{0,2},{1,3},{2,0},{3,1},{4,6},{5,7},{6,4},{7,5},{8,10},{9,11},{10,... | collective-permute-start | bytes 3145736 | tf_op jit(solution)/shard_map/ppermute | solution.py:17
  110.8 24.7 %collective-permute-start.2 = (f32[512,512]{1,0:T(8,128)S(1)}, f32[512,512]{1,0:T(8,128)S(1)}, u32[]{:S(2)}, u32[]{:S(2)}) collective-permute-start(f32[512,512]{1,0:T(8,128)S(1)} %add.77), channel_id=1, source_target_pairs={{0,4},{1,5},{2,6},{3,7},{4,0},{5,1},{6,2},{7,3},{8,12},{9,13},{10,... | collective-permute-start | bytes 3145736 | tf_op jit(solution)/shard_map/ppermute | solution.py:17
  137.0 2.7 %collective-permute-start.3 = (f32[512,512]{1,0:T(8,128)S(1)}, f32[512,512]{1,0:T(8,128)S(1)}, u32[]{:S(2)}, u32[]{:S(2)}) collective-permute-start(f32[512,512]{1,0:T(8,128)S(1)} %fusion.23), channel_id=1, source_target_pairs={{0,1},{1,0},{2,3},{3,2},{4,5},{5,4},{6,7},{7,6},{8,9},{9,8},{10,11... | collective-permute-start | bytes 3145736 | tf_op jit(solution)/shard_map/ppermute | solution.py:17
  139.9 25.3 %collective-permute-start.4 = (f32[512,512]{1,0:T(8,128)S(1)}, f32[512,512]{1,0:T(8,128)S(1)}, u32[]{:S(2)}, u32[]{:S(2)}) collective-permute-start(f32[512,512]{1,0:T(8,128)S(1)} %add.81), channel_id=1, source_target_pairs={{0,2},{1,3},{2,0},{3,1},{4,6},{5,7},{6,4},{7,5},{8,10},{9,11},{10,... | collective-permute-start | bytes 3145736 | tf_op jit(solution)/shard_map/ppermute | solution.py:17
  165.4 24.4 %collective-permute-start.5 = (f32[512,512]{1,0:T(8,128)S(1)}, f32[512,512]{1,0:T(8,128)S(1)}, u32[]{:S(2)}, u32[]{:S(2)}) collective-permute-start(f32[512,512]{1,0:T(8,128)S(1)} %add.82), channel_id=1, source_target_pairs={{0,4},{1,5},{2,6},{3,7},{4,0},{5,1},{6,2},{7,3},{8,12},{9,13},{10,... | collective-permute-start | bytes 3145736 | tf_op jit(solution)/shard_map/ppermute | solution.py:17
  191.3 2.7 %collective-permute-start.6 = (f32[512,512]{1,0:T(8,128)S(1)}, f32[512,512]{1,0:T(8,128)S(1)}, u32[]{:S(2)}, u32[]{:S(2)}) collective-permute-start(f32[512,512]{1,0:T(8,128)S(1)} %fusion.24), channel_id=1, source_target_pairs={{0,1},{1,0},{2,3},{3,2},{4,5},{5,4},{6,7},{7,6},{8,9},{9,8},{10,11... | collective-permute-start | bytes 3145736 | tf_op jit(solution)/shard_map/ppermute | solution.py:17
  194.2 25.3 %collective-permute-start.7 = (f32[512,512]{1,0:T(8,128)S(1)}, f32[512,512]{1,0:T(8,128)S(1)}, u32[]{:S(2)}, u32[]{:S(2)}) collective-permute-start(f32[512,512]{1,0:T(8,128)S(1)} %add.86), channel_id=1, source_target_pairs={{0,2},{1,3},{2,0},{3,1},{4,6},{5,7},{6,4},{7,5},{8,10},{9,11},{10,... | collective-permute-start | bytes 3145736 | tf_op jit(solution)/shard_map/ppermute | solution.py:17
  219.7 24.4 %collective-permute-start.8 = (f32[512,512]{1,0:T(8,128)S(1)}, f32[512,512]{1,0:T(8,128)S(1)}, u32[]{:S(2)}, u32[]{:S(2)}) collective-permute-start(f32[512,512]{1,0:T(8,128)S(1)} %add.87), channel_id=1, source_target_pairs={{0,4},{1,5},{2,6},{3,7},{4,0},{5,1},{6,2},{7,3},{8,12},{9,13},{10,... | collective-permute-start | bytes 3145736 | tf_op jit(solution)/shard_map/ppermute | solution.py:17
  245.9 18.7 %all-to-all-start.2 = ((bf16[1,16,32,512]{3,2,0,1:T(8,128)(2,1)}), bf16[1,16,32,512]{3,2,0,1:T(8,128)(2,1)S(1)}, u32[]{:S(2)}, u32[]{:S(2)}) async-start(bf16[1,16,32,512]{3,2,0,1:T(8,128)(2,1)} %bitcast.5), calls=%async_computation.2 | async-start | bytes 1048576 | tf_op jit(solution)/shard_map/all_to_all | solution.py:102
where the time goes:
time: 266 us
  waiting for transfers between devices  172 us (65%)
  blocking collectives  59.3 us (22%)
  starting transfers between devices  18.3 us (7%)
  other arithmetic  9.43 us (4%)
  matrix products  4.55 us (2%)
    ppermute x9, waiting for transfers between devices, partner(): lax.ppermute(shard, axis, [(i, i ^ 1 << stride) for i in range(lax.axis_s...  148 us
    psum x1, blocking collectives, share_scores(): return lax.psum((aligned, squares, norm_slots), ('domain', 'fsdp'))  39.8 us
    all_to_all x1, blocking collectives, body(): lax.all_to_all(scaled, 'fsdp', split_axis=0, concat_axis=1, tiled=True)  19.5 us
    all_to_all x1, waiting for transfers between devices, body(): lax.all_to_all(gradients.reshape(1, groups, per_domain, rows_src, columns...  12.7 us
    all_to_all x1, waiting for transfers between devices, body(): lax.all_to_all(finished.reshape(1, shards, sub_rows, columns), 'fsdp', sp...  11.6 us
    ppermute x9, starting transfers between devices, partner(): lax.ppermute(shard, axis, [(i, i ^ 1 << stride) for i in range(lax.axis_s...  9.5 us
  transfers between devices with their start and end apart: 11, of which 11 were waited for; matrix products, arithmetic and copies ran while one was open for 2% of the time, Pallas kernels for 0%

commit v1 on v0

--- a/solution.py
+++ b/solution.py
@@ -11,6 +11,17 @@
 COEF_C = 2.0315
 MUON_SCALE = 0.2
 ETA = 4.0
+
+
+def split_up(x, dim, devices):
+    before, after = (x.shape[:dim], x.shape[dim + 1 :])
+    return jnp.moveaxis(x.reshape(*before, devices, -1, *after), dim, 0)
+
+
+def laid_out(parts, dim):
+    shape = list(parts.shape[1:])
+    shape[dim] *= parts.shape[0]
+    return jnp.moveaxis(parts, 0, dim).reshape(shape)
 
 
 def partner(shard, axis, stride):
@@ -96,7 +107,14 @@
     )
     scaled = (combined / frob_norm[:, None, None]).astype(jnp.bfloat16)
     scaled = scaled.reshape(shards, 1, sub_rows, columns)
-    start_rows = lax.all_to_all(scaled, "fsdp", split_axis=0, concat_axis=1, tiled=True)
+    size, position = (lax.axis_size("fsdp"), lax.axis_index("fsdp"))
+    parts = split_up(scaled, 0, size)
+    outs = [parts[position]]
+    for hop in range(1, size):
+        sent = parts[position ^ hop]
+        outs.append(lax.ppermute(sent, "fsdp", [(i_2, i_2 ^ hop) for i_2 in range(size)]))
+    parts = jnp.stack(outs)[position ^ jnp.arange(size)]
+    start_rows = laid_out(parts, 1)
     start_rows = lax.optimization_barrier(start_rows.reshape(own_rows, columns))
     finished = newton_steps(start_rows)
     returned = lax.all_to_all(

time: 266 us -> 300 us (1.13)
  waiting for transfers between devices: 172 us -> 214 us
  blocking collectives: 59.3 us -> 39.8 us
  starting transfers between devices: 18.3 us -> 29.3 us
    ppermute x0 -> x15, waiting for transfers between devices: none -> 36.8 us  [body(): lax.ppermute(sent, 'fsdp', [(i_2, i_2 ^ hop) for i_2 in range(size)])]
    all_to_all x1 -> x0, blocking collectives: 19.5 us -> none  [body(): lax.all_to_all(scaled, 'fsdp', split_axis=0, concat_axis=1, tiled=True)]
    ppermute x0 -> x15, starting transfers between devices: none -> 16.2 us  [body(): lax.ppermute(sent, 'fsdp', [(i_2, i_2 ^ hop) for i_2 in range(size)])]
    ppermute x9, starting transfers between devices: 9.5 us -> 4.74 us  [partner(): lax.ppermute(shard, axis, [(i, i ^ 1 << stride) for i in range(lax.axis_s...]
    ppermute x9, waiting for transfers between devices: 148 us -> 152 us  [partner(): lax.ppermute(shard, axis, [(i, i ^ 1 << stride) for i in range(lax.axis_s...]
  transfers between devices with their start and end apart: 11 -> 26, of which waited for: 11 -> 21; matrix products, arithmetic and copies ran while one was open for 2% -> 1% of each run, Pallas kernels for 0% -> 0%
where the time goes in v1:
time: 300 us; the launch traced here: 299 us
  waiting for transfers between devices  214 us (71%)
  blocking collectives  39.8 us (13%)
  starting transfers between devices  29.3 us (10%)
  other arithmetic  9.3 us (3%)
  matrix products  4.54 us (2%)
    ppermute x9, waiting for transfers between devices, partner(): lax.ppermute(shard, axis, [(i, i ^ 1 << stride) for i in range(lax.axis_s...  152 us
    psum x1, blocking collectives, share_scores(): return lax.psum((aligned, squares, norm_slots), ('domain', 'fsdp'))  39.8 us
    ppermute x15, waiting for transfers between devices, body(): lax.ppermute(sent, 'fsdp', [(i_2, i_2 ^ hop) for i_2 in range(size)])  36.8 us
    ppermute x15, starting transfers between devices, body(): lax.ppermute(sent, 'fsdp', [(i_2, i_2 ^ hop) for i_2 in range(size)])  16.2 us
    all_to_all x1, waiting for transfers between devices, body(): lax.all_to_all(gradients.reshape(1, groups, per_domain, rows_src, columns...  12.7 us
    all_to_all x1, waiting for transfers between devices, body(): lax.all_to_all(finished.reshape(1, shards, sub_rows, columns), 'fsdp', sp...  11.8 us
  transfers between devices with their start and end apart: 26, of which 21 were waited for; matrix products, arithmetic and copies ran while one was open for 1% of the time, Pallas kernels for 0%

profile of v1, /device:TPU:0, one launch (start us, length us, event | category | flops | bytes accessed | tf_op | source)
XLA Modules:
  0.0 299.4 jit_solution(16418024474063414166)
XLA Ops:
  0.7 4.4 %all-to-all-start = ((bf16[1,2,2,256,512]{4,3,2,0,1:T(8,128)(2,1)}), bf16[1,2,2,256,512]{4,3,2,0,1:T(8,128)(2,1)S(1)}, u32[]{:S(2)}, u32[]{:S(2)}) async-start(bf16[1,2,2,256,512]{4,3,2,0,1:T(8,128)(2,1)} %bitcast.94), calls=%async_computation | async-start | bytes 2097152 | tf_op jit(solution)/shard_map/all_to_all | solution.py:84
  5.2 0.6 reduce_sum.92
  5.9 0.7 multiply_divide_fusion
  6.8 12.7 %all-to-all-done = bf16[1,2,2,256,512]{4,3,2,0,1:T(8,128)(2,1)S(1)} async-done(((bf16[1,2,2,256,512]{4,3,2,0,1:T(8,128)(2,1)}), bf16[1,2,2,256,512]{4,3,2,0,1:T(8,128)(2,1)S(1)}, u32[]{:S(2)}, u32[]{:S(2)}) %all-to-all-start) | async-done | bytes 1048608 | tf_op jit(solution)/shard_map/all_to_all | solution.py:84
  19.5 0.3 fusion.3
  19.8 0.2 multiply_reduce_fusion
  20.2 0.7 fusion.5
  20.9 39.8 %all-reduce = (f32[4]{0:T(128)S(1)}, f32[2]{0:T(128)S(1)}, f32[2]{0:T(128)S(1)}) all-reduce(f32[4]{0:T(128)S(1)} %dynamic_update_slice.3, f32[2]{0:T(128)S(1)} %get-tuple-element.3, f32[2]{0:T(128)S(1)} %get-tuple-element.2), channel_id=1, replica_groups=mesh['domain'=2,'fsdp'=16] {'domain','fsdp'}, use_global_device_ids=true, to_apply=%region_5.6 | all-reduce | flops 8 | bytes 64 | tf_op jit(solution)/shard_map/psum | solution.py:66
  60.7 0.6 reduce_sum.100
  62.6 4.0 %collective-permute-start.14 = (bf16[1,1,32,512]{3,2,1,0:T(8,128)(2,1)S(1)}, bf16[1,1,32,512]{3,2,1,0:T(8,128)(2,1)S(1)}, u32[]{:S(2)}, u32[]{:S(2)}) collective-permute-start(bf16[1,1,32,512]{3,2,1,0:T(8,128)(2,1)S(1)} %get-tuple-element.9), channel_id=1, source_target_pairs={{0,15},{1,14},{2,13},{3,12},{4,11},{5,10},{6,9},{7,8},{8,7},{9,6},... | collective-permute-start | bytes 98312 | tf_op jit(solution)/shard_map/ppermute | solution.py:115
  66.6 0.8 collective-permute-start.13
  67.4 1.6 collective-permute-start.12
  69.0 1.6 collective-permute-start.11
  70.7 2.3 collective-permute-start.1
  72.9 2.0 collective-permute-done.1
  74.9 1.1 collective-permute-start.2
  76.0 2.2 collective-permute-done.2
  78.3 3.9 %collective-permute-done.3 = bf16[1,1,32,512]{3,2,1,0:T(8,128)(2,1)S(1)} collective-permute-done((bf16[1,1,32,512]{3,2,1,0:T(8,128)(2,1)S(1)}, bf16[1,1,32,512]{3,2,1,0:T(8,128)(2,1)S(1)}, u32[]{:S(2)}, u32[]{:S(2)}) %collective-permute-start.3) | collective-permute-done | bytes 32800 | tf_op jit(solution)/shard_map/ppermute | solution.py:115
  82.2 3.3 %collective-permute-done.4 = bf16[1,1,32,512]{3,2,1,0:T(8,128)(2,1)S(1)} collective-permute-done((bf16[1,1,32,512]{3,2,1,0:T(8,128)(2,1)S(1)}, bf16[1,1,32,512]{3,2,1,0:T(8,128)(2,1)S(1)}, u32[]{:S(2)}, u32[]{:S(2)}) %collective-permute-start.4) | collective-permute-done | bytes 32800 | tf_op jit(solution)/shard_map/ppermute | solution.py:115
  85.5 1.5 collective-permute-start.5
  87.0 3.3 %collective-permute-done.5 = bf16[1,1,32,512]{3,2,1,0:T(8,128)(2,1)S(1)} collective-permute-done((bf16[1,1,32,512]{3,2,1,0:T(8,128)(2,1)S(1)}, bf16[1,1,32,512]{3,2,1,0:T(8,128)(2,1)S(1)}, u32[]{:S(2)}, u32[]{:S(2)}) %collective-permute-start.5) | collective-permute-done | bytes 32800 | tf_op jit(solution)/shard_map/ppermute | solution.py:115
  90.3 0.3 collective-permute-start.6
  90.7 3.9 %collective-permute-done.6 = bf16[1,1,32,512]{3,2,1,0:T(8,128)(2,1)S(1)} collective-permute-done((bf16[1,1,32,512]{3,2,1,0:T(8,128)(2,1)S(1)}, bf16[1,1,32,512]{3,2,1,0:T(8,128)(2,1)S(1)}, u32[]{:S(2)}, u32[]{:S(2)}) %collective-permute-start.6) | collective-permute-done | bytes 32800 | tf_op jit(solution)/shard_map/ppermute | solution.py:115
  94.6 1.3 collective-permute-start.7
  95.9 3.8 %collective-permute-done.7 = bf16[1,1,32,512]{3,2,1,0:T(8,128)(2,1)S(1)} collective-permute-done((bf16[1,1,32,512]{3,2,1,0:T(8,128)(2,1)S(1)}, bf16[1,1,32,512]{3,2,1,0:T(8,128)(2,1)S(1)}, u32[]{:S(2)}, u32[]{:S(2)}) %collective-permute-start.7) | collective-permute-done | bytes 32800 | tf_op jit(solution)/shard_map/ppermute | solution.py:115
  99.7 4.7 %collective-permute-done.8 = bf16[1,1,32,512]{3,2,1,0:T(8,128)(2,1)S(1)} collective-permute-done((bf16[1,1,32,512]{3,2,1,0:T(8,128)(2,1)S(1)}, bf16[1,1,32,512]{3,2,1,0:T(8,128)(2,1)S(1)}, u32[]{:S(2)}, u32[]{:S(2)}) %collective-permute-start.8) | collective-permute-done | bytes 32800 | tf_op jit(solution)/shard_map/ppermute | solution.py:115
  104.4 1.6 collective-permute-start.9
  106.0 4.1 %collective-permute-done.9 = bf16[1,1,32,512]{3,2,1,0:T(8,128)(2,1)S(1)} collective-permute-done((bf16[1,1,32,512]{3,2,1,0:T(8,128)(2,1)S(1)}, bf16[1,1,32,512]{3,2,1,0:T(8,128)(2,1)S(1)}, u32[]{:S(2)}, u32[]{:S(2)}) %collective-permute-start.9) | collective-permute-done | bytes 32800 | tf_op jit(solution)/shard_map/ppermute | solution.py:115
  110.2 5.4 %collective-permute-done.10 = bf16[1,1,32,512]{3,2,1,0:T(8,128)(2,1)S(1)} collective-permute-done((bf16[1,1,32,512]{3,2,1,0:T(8,128)(2,1)S(1)}, bf16[1,1,32,512]{3,2,1,0:T(8,128)(2,1)S(1)}, u32[]{:S(2)}, u32[]{:S(2)}) %collective-permute-start.10) | collective-permute-done | bytes 32800 | tf_op jit(solution)/shard_map/ppermute | solution.py:115
  115.7 0.6 gather_fusion
  116.3 0.5 fusion.23
  116.8 2.6 collective-permute-done.15
  119.5 0.2 add.151
  119.7 1.2 collective-permute-start.16
  120.9 24.1 %collective-permute-done.16 = f32[512,512]{1,0:T(8,128)S(1)} collective-permute-done((f32[512,512]{1,0:T(8,128)S(1)}, f32[512,512]{1,0:T(8,128)S(1)}, u32[]{:S(2)}, u32[]{:S(2)}) %collective-permute-start.16) | collective-permute-done | bytes 1048608 | tf_op jit(solution)/shard_map/ppermute | solution.py:28
  144.9 0.2 add.152
  145.2 0.3 collective-permute-start.17
  145.4 24.1 %collective-permute-done.17 = f32[512,512]{1,0:T(8,128)S(1)} collective-permute-done((f32[512,512]{1,0:T(8,128)S(1)}, f32[512,512]{1,0:T(8,128)S(1)}, u32[]{:S(2)}, u32[]{:S(2)}) %collective-permute-start.17) | collective-permute-done | bytes 1048608 | tf_op jit(solution)/shard_map/ppermute | solution.py:28
  169.6 0.3 add_convert_fusion.5
  169.8 0.8 fusion.6
  170.6 0.5 fusion.24
  171.2 2.6 collective-permute-done.18
  173.8 0.2 add.156
  174.0 1.2 collective-permute-start.19
  175.2 24.1 %collective-permute-done.19 = f32[512,512]{1,0:T(8,128)S(1)} collective-permute-done((f32[512,512]{1,0:T(8,128)S(1)}, f32[512,512]{1,0:T(8,128)S(1)}, u32[]{:S(2)}, u32[]{:S(2)}) %collective-permute-start.19) | collective-permute-done | bytes 1048608 | tf_op jit(solution)/shard_map/ppermute | solution.py:28
  199.3 0.2 add.157
  199.5 0.4 collective-permute-start.20
  199.8 24.1 %collective-permute-done.20 = f32[512,512]{1,0:T(8,128)S(1)} collective-permute-done((f32[512,512]{1,0:T(8,128)S(1)}, f32[512,512]{1,0:T(8,128)S(1)}, u32[]{:S(2)}, u32[]{:S(2)}) %collective-permute-start.20) | collective-permute-done | bytes 1048608 | tf_op jit(solution)/shard_map/ppermute | solution.py:28
  223.9 0.3 add_convert_fusion.3
  224.2 0.8 fusion.7
  224.9 0.5 fusion.25
  225.5 2.6 collective-permute-done.21
  228.1 0.2 add.161
  228.4 1.2 collective-permute-start.22
  229.5 24.1 %collective-permute-done.22 = f32[512,512]{1,0:T(8,128)S(1)} collective-permute-done((f32[512,512]{1,0:T(8,128)S(1)}, f32[512,512]{1,0:T(8,128)S(1)}, u32[]{:S(2)}, u32[]{:S(2)}) %collective-permute-start.22) | collective-permute-done | bytes 1048608 | tf_op jit(solution)/shard_map/ppermute | solution.py:28
  253.8 0.4 collective-permute-start.23
  254.2 24.1 %collective-permute-done.23 = f32[512,512]{1,0:T(8,128)S(1)} collective-permute-done((f32[512,512]{1,0:T(8,128)S(1)}, f32[512,512]{1,0:T(8,128)S(1)}, u32[]{:S(2)}, u32[]{:S(2)}) %collective-permute-start.23) | collective-permute-done | bytes 1048608 | tf_op jit(solution)/shard_map/ppermute | solution.py:28
  278.2 0.3 add_convert_fusion.1
  278.5 1.6 fusion.8
  280.1 3.9 %all-to-all-start.1 = ((bf16[1,16,32,512]{3,2,0,1:T(8,128)(2,1)}), bf16[1,16,32,512]{3,2,0,1:T(8,128)(2,1)S(1)}, u32[]{:S(2)}, u32[]{:S(2)}) async-start(bf16[1,16,32,512]{3,2,0,1:T(8,128)(2,1)} %bitcast.37), calls=%async_computation.1 | async-start | bytes 1048576 | tf_op jit(solution)/shard_map/all_to_all | solution.py:120
  284.1 1.3 fusion.22
  285.4 1.1 broadcast_divide_fusion
  286.5 11.8 %all-to-all-done.1 = bf16[1,16,32,512]{3,2,0,1:T(8,128)(2,1)S(1)} async-done(((bf16[1,16,32,512]{3,2,0,1:T(8,128)(2,1)}), bf16[1,16,32,512]{3,2,0,1:T(8,128)(2,1)S(1)}, u32[]{:S(2)}, u32[]{:S(2)}) %all-to-all-start.1) | async-done | bytes 524320 | tf_op jit(solution)/shard_map/all_to_all | solution.py:120
  298.3 1.1 convert_multiply_fusion
  (50 shorter events, 1.8 us)
Async XLA Ops:
  0.6 4.4 %copy-start.2 = (s32[2]{0:T(128)S(1)}, s32[2]{0:T(128)}, u32[]{:S(2)}) copy-start(s32[2]{0:T(128)} %param.6) | copy-start | bytes 28
  0.6 4.6 %copy-start = (f32[8]{0:T(128)S(1)}, f32[8]{0:T(128)}, u32[]{:S(2)}) copy-start(f32[8]{0:T(128)} %param.7) | copy-start | bytes 100
  0.7 5.2 %copy-start.1 = (s32[4]{0:T(128)S(1)}, s32[4]{0:T(128)}, u32[]{:S(2)}) copy-start(s32[4]{0:T(128)} %param.5) | copy-start | bytes 52
  0.7 18.8 %all-to-all-start = ((bf16[1,2,2,256,512]{4,3,2,0,1:T(8,128)(2,1)}), bf16[1,2,2,256,512]{4,3,2,0,1:T(8,128)(2,1)S(1)}, u32[]{:S(2)}, u32[]{:S(2)}) async-start(bf16[1,2,2,256,512]{4,3,2,0,1:T(8,128)(2,1)} %bitcast.94), calls=%async_computation | async-start | bytes 2097152 | tf_op jit(solution)/shard_map/all_to_all | solution.py:84
  62.5 8.1 %collective-permute-start = (bf16[1,1,32,512]{3,2,1,0:T(8,128)(2,1)S(1)}, bf16[1,1,32,512]{3,2,1,0:T(8,128)(2,1)S(1)}, u32[]{:S(2)}, u32[]{:S(2)}) collective-permute-start(bf16[1,1,32,512]{3,2,1,0:T(8,128)(2,1)S(1)} %get-tuple-element.23), channel_id=1, source_target_pairs={{0,1},{1,0},{2,3},{3,2},{4,5},{5,4},{6,7},{7,6},{8,9},{9,8},{10,11... | collective-permute-start | bytes 98312 | tf_op jit(solution)/shard_map/ppermute | solution.py:115
  62.6 53.0 %collective-permute-start.14 = (bf16[1,1,32,512]{3,2,1,0:T(8,128)(2,1)S(1)}, bf16[1,1,32,512]{3,2,1,0:T(8,128)(2,1)S(1)}, u32[]{:S(2)}, u32[]{:S(2)}) collective-permute-start(bf16[1,1,32,512]{3,2,1,0:T(8,128)(2,1)S(1)} %get-tuple-element.9), channel_id=1, source_target_pairs={{0,15},{1,14},{2,13},{3,12},{4,11},{5,10},{6,9},{7,8},{8,7},{9,6},... | collective-permute-start | bytes 98312 | tf_op jit(solution)/shard_map/ppermute | solution.py:115
  66.6 49.0 %collective-permute-start.13 = (bf16[1,1,32,512]{3,2,1,0:T(8,128)(2,1)S(1)}, bf16[1,1,32,512]{3,2,1,0:T(8,128)(2,1)S(1)}, u32[]{:S(2)}, u32[]{:S(2)}) collective-permute-start(bf16[1,1,32,512]{3,2,1,0:T(8,128)(2,1)S(1)} %get-tuple-element.10), channel_id=1, source_target_pairs={{0,14},{1,15},{2,12},{3,13},{4,10},{5,11},{6,8},{7,9},{8,6},{9,7},... | collective-permute-start | bytes 98312 | tf_op jit(solution)/shard_map/ppermute | solution.py:115
  67.4 48.2 %collective-permute-start.12 = (bf16[1,1,32,512]{3,2,1,0:T(8,128)(2,1)S(1)}, bf16[1,1,32,512]{3,2,1,0:T(8,128)(2,1)S(1)}, u32[]{:S(2)}, u32[]{:S(2)}) collective-permute-start(bf16[1,1,32,512]{3,2,1,0:T(8,128)(2,1)S(1)} %get-tuple-element.11), channel_id=1, source_target_pairs={{0,13},{1,12},{2,15},{3,14},{4,9},{5,8},{6,11},{7,10},{8,5},{9,4},... | collective-permute-start | bytes 98312 | tf_op jit(solution)/shard_map/ppermute | solution.py:115
  69.0 46.6 %collective-permute-start.11 = (bf16[1,1,32,512]{3,2,1,0:T(8,128)(2,1)S(1)}, bf16[1,1,32,512]{3,2,1,0:T(8,128)(2,1)S(1)}, u32[]{:S(2)}, u32[]{:S(2)}) collective-permute-start(bf16[1,1,32,512]{3,2,1,0:T(8,128)(2,1)S(1)} %get-tuple-element.12), channel_id=1, source_target_pairs={{0,12},{1,13},{2,14},{3,15},{4,8},{5,9},{6,10},{7,11},{8,4},{9,5},... | collective-permute-start | bytes 98312 | tf_op jit(solution)/shard_map/ppermute | solution.py:115
  70.7 4.2 %collective-permute-start.1 = (bf16[1,1,32,512]{3,2,1,0:T(8,128)(2,1)S(1)}, bf16[1,1,32,512]{3,2,1,0:T(8,128)(2,1)S(1)}, u32[]{:S(2)}, u32[]{:S(2)}) collective-permute-start(bf16[1,1,32,512]{3,2,1,0:T(8,128)(2,1)S(1)} %get-tuple-element.22), channel_id=1, source_target_pairs={{0,2},{1,3},{2,0},{3,1},{4,6},{5,7},{6,4},{7,5},{8,10},{9,11},{10,... | collective-permute-start | bytes 98312 | tf_op jit(solution)/shard_map/ppermute | solution.py:115
  74.9 3.3 %collective-permute-start.2 = (bf16[1,1,32,512]{3,2,1,0:T(8,128)(2,1)S(1)}, bf16[1,1,32,512]{3,2,1,0:T(8,128)(2,1)S(1)}, u32[]{:S(2)}, u32[]{:S(2)}) collective-permute-start(bf16[1,1,32,512]{3,2,1,0:T(8,128)(2,1)S(1)} %get-tuple-element.21), channel_id=1, source_target_pairs={{0,3},{1,2},{2,1},{3,0},{4,7},{5,6},{6,5},{7,4},{8,11},{9,10},{10,... | collective-permute-start | bytes 98312 | tf_op jit(solution)/shard_map/ppermute | solution.py:115
  78.3 3.9 %collective-permute-start.3 = (bf16[1,1,32,512]{3,2,1,0:T(8,128)(2,1)S(1)}, bf16[1,1,32,512]{3,2,1,0:T(8,128)(2,1)S(1)}, u32[]{:S(2)}, u32[]{:S(2)}) collective-permute-start(bf16[1,1,32,512]{3,2,1,0:T(8,128)(2,1)S(1)} %get-tuple-element.20), channel_id=1, source_target_pairs={{0,4},{1,5},{2,6},{3,7},{4,0},{5,1},{6,2},{7,3},{8,12},{9,13},{10,... | collective-permute-start | bytes 98312 | tf_op jit(solution)/shard_map/ppermute | solution.py:115
  82.2 3.3 %collective-permute-start.4 = (bf16[1,1,32,512]{3,2,1,0:T(8,128)(2,1)S(1)}, bf16[1,1,32,512]{3,2,1,0:T(8,128)(2,1)S(1)}, u32[]{:S(2)}, u32[]{:S(2)}) collective-permute-start(bf16[1,1,32,512]{3,2,1,0:T(8,128)(2,1)S(1)} %get-tuple-element.19), channel_id=1, source_target_pairs={{0,5},{1,4},{2,7},{3,6},{4,1},{5,0},{6,3},{7,2},{8,13},{9,12},{10,... | collective-permute-start | bytes 98312 | tf_op jit(solution)/shard_map/ppermute | solution.py:115
  85.5 4.8 %collective-permute-start.5 = (bf16[1,1,32,512]{3,2,1,0:T(8,128)(2,1)S(1)}, bf16[1,1,32,512]{3,2,1,0:T(8,128)(2,1)S(1)}, u32[]{:S(2)}, u32[]{:S(2)}) collective-permute-start(bf16[1,1,32,512]{3,2,1,0:T(8,128)(2,1)S(1)} %get-tuple-element.18), channel_id=1, source_target_pairs={{0,6},{1,7},{2,4},{3,5},{4,2},{5,3},{6,0},{7,1},{8,14},{9,15},{10,... | collective-permute-start | bytes 98312 | tf_op jit(solution)/shard_map/ppermute | solution.py:115
  90.3 4.2 %collective-permute-start.6 = (bf16[1,1,32,512]{3,2,1,0:T(8,128)(2,1)S(1)}, bf16[1,1,32,512]{3,2,1,0:T(8,128)(2,1)S(1)}, u32[]{:S(2)}, u32[]{:S(2)}) collective-permute-start(bf16[1,1,32,512]{3,2,1,0:T(8,128)(2,1)S(1)} %get-tuple-element.17), channel_id=1, source_target_pairs={{0,7},{1,6},{2,5},{3,4},{4,3},{5,2},{6,1},{7,0},{8,15},{9,14},{10,... | collective-permute-start | bytes 98312 | tf_op jit(solution)/shard_map/ppermute | solution.py:115
  94.6 5.2 %collective-permute-start.7 = (bf16[1,1,32,512]{3,2,1,0:T(8,128)(2,1)S(1)}, bf16[1,1,32,512]{3,2,1,0:T(8,128)(2,1)S(1)}, u32[]{:S(2)}, u32[]{:S(2)}) collective-permute-start(bf16[1,1,32,512]{3,2,1,0:T(8,128)(2,1)S(1)} %get-tuple-element.16), channel_id=1, source_target_pairs={{0,8},{1,9},{2,10},{3,11},{4,12},{5,13},{6,14},{7,15},{8,0},{9,1},... | collective-permute-start | bytes 98312 | tf_op jit(solution)/shard_map/ppermute | solution.py:115
  99.7 4.7 %collective-permute-start.8 = (bf16[1,1,32,512]{3,2,1,0:T(8,128)(2,1)S(1)}, bf16[1,1,32,512]{3,2,1,0:T(8,128)(2,1)S(1)}, u32[]{:S(2)}, u32[]{:S(2)}) collective-permute-start(bf16[1,1,32,512]{3,2,1,0:T(8,128)(2,1)S(1)} %get-tuple-element.15), channel_id=1, source_target_pairs={{0,9},{1,8},{2,11},{3,10},{4,13},{5,12},{6,15},{7,14},{8,1},{9,0},... | collective-permute-start | bytes 98312 | tf_op jit(solution)/shard_map/ppermute | solution.py:115
  104.4 5.7 %collective-permute-start.9 = (bf16[1,1,32,512]{3,2,1,0:T(8,128)(2,1)S(1)}, bf16[1,1,32,512]{3,2,1,0:T(8,128)(2,1)S(1)}, u32[]{:S(2)}, u32[]{:S(2)}) collective-permute-start(bf16[1,1,32,512]{3,2,1,0:T(8,128)(2,1)S(1)} %get-tuple-element.14), channel_id=1, source_target_pairs={{0,10},{1,11},{2,8},{3,9},{4,14},{5,15},{6,12},{7,13},{8,2},{9,3},... | collective-permute-start | bytes 98312 | tf_op jit(solution)/shard_map/ppermute | solution.py:115
  110.1 5.4 %collective-permute-start.10 = (bf16[1,1,32,512]{3,2,1,0:T(8,128)(2,1)S(1)}, bf16[1,1,32,512]{3,2,1,0:T(8,128)(2,1)S(1)}, u32[]{:S(2)}, u32[]{:S(2)}) collective-permute-start(bf16[1,1,32,512]{3,2,1,0:T(8,128)(2,1)S(1)} %get-tuple-element.13), channel_id=1, source_target_pairs={{0,11},{1,10},{2,9},{3,8},{4,15},{5,14},{6,13},{7,12},{8,3},{9,2},... | collective-permute-start | bytes 98312 | tf_op jit(solution)/shard_map/ppermute | solution.py:115
  116.7 2.7 collective-permute-start.15
  119.7 25.3 %collective-permute-start.16 = (f32[512,512]{1,0:T(8,128)S(1)}, f32[512,512]{1,0:T(8,128)S(1)}, u32[]{:S(2)}, u32[]{:S(2)}) collective-permute-start(f32[512,512]{1,0:T(8,128)S(1)} %add.151), channel_id=1, source_target_pairs={{0,2},{1,3},{2,0},{3,1},{4,6},{5,7},{6,4},{7,5},{8,10},{9,11},{10,... | collective-permute-start | bytes 3145736 | tf_op jit(solution)/shard_map/ppermute | solution.py:28
  145.2 24.4 %collective-permute-start.17 = (f32[512,512]{1,0:T(8,128)S(1)}, f32[512,512]{1,0:T(8,128)S(1)}, u32[]{:S(2)}, u32[]{:S(2)}) collective-permute-start(f32[512,512]{1,0:T(8,128)S(1)} %add.152), channel_id=1, source_target_pairs={{0,4},{1,5},{2,6},{3,7},{4,0},{5,1},{6,2},{7,3},{8,12},{9,13},{10,... | collective-permute-start | bytes 3145736 | tf_op jit(solution)/shard_map/ppermute | solution.py:28
  171.1 2.7 collective-permute-start.18
  174.0 25.3 %collective-permute-start.19 = (f32[512,512]{1,0:T(8,128)S(1)}, f32[512,512]{1,0:T(8,128)S(1)}, u32[]{:S(2)}, u32[]{:S(2)}) collective-permute-start(f32[512,512]{1,0:T(8,128)S(1)} %add.156), channel_id=1, source_target_pairs={{0,2},{1,3},{2,0},{3,1},{4,6},{5,7},{6,4},{7,5},{8,10},{9,11},{10,... | collective-permute-start | bytes 3145736 | tf_op jit(solution)/shard_map/ppermute | solution.py:28
  199.5 24.4 %collective-permute-start.20 = (f32[512,512]{1,0:T(8,128)S(1)}, f32[512,512]{1,0:T(8,128)S(1)}, u32[]{:S(2)}, u32[]{:S(2)}) collective-permute-start(f32[512,512]{1,0:T(8,128)S(1)} %add.157), channel_id=1, source_target_pairs={{0,4},{1,5},{2,6},{3,7},{4,0},{5,1},{6,2},{7,3},{8,12},{9,13},{10,... | collective-permute-start | bytes 3145736 | tf_op jit(solution)/shard_map/ppermute | solution.py:28
  225.4 2.7 collective-permute-start.21
  228.4 25.3 %collective-permute-start.22 = (f32[512,512]{1,0:T(8,128)S(1)}, f32[512,512]{1,0:T(8,128)S(1)}, u32[]{:S(2)}, u32[]{:S(2)}) collective-permute-start(f32[512,512]{1,0:T(8,128)S(1)} %add.161), channel_id=1, source_target_pairs={{0,2},{1,3},{2,0},{3,1},{4,6},{5,7},{6,4},{7,5},{8,10},{9,11},{10,... | collective-permute-start | bytes 3145736 | tf_op jit(solution)/shard_map/ppermute | solution.py:28
  253.8 24.4 %collective-permute-start.23 = (f32[512,512]{1,0:T(8,128)S(1)}, f32[512,512]{1,0:T(8,128)S(1)}, u32[]{:S(2)}, u32[]{:S(2)}) collective-permute-start(f32[512,512]{1,0:T(8,128)S(1)} %add.162), channel_id=1, source_target_pairs={{0,4},{1,5},{2,6},{3,7},{4,0},{5,1},{6,2},{7,3},{8,12},{9,13},{10,... | collective-permute-start | bytes 3145736 | tf_op jit(solution)/shard_map/ppermute | solution.py:28
  280.1 18.2 %all-to-all-start.1 = ((bf16[1,16,32,512]{3,2,0,1:T(8,128)(2,1)}), bf16[1,16,32,512]{3,2,0,1:T(8,128)(2,1)S(1)}, u32[]{:S(2)}, u32[]{:S(2)}) async-start(bf16[1,16,32,512]{3,2,0,1:T(8,128)(2,1)} %bitcast.37), calls=%async_computation.1 | async-start | bytes 1048576 | tf_op jit(solution)/shard_map/all_to_all | solution.py:120
